TPU v7x, 32 devices: a whole 2x2x4 slice. The times are simulated.
32 devices in a mesh: event: 8 (over z, x), lon: 4 (over y, core).
Axes of the slice: x: 2, y: 2, z: 4, core: 2. Of those that a mesh axis runs over, the one named last changes fastest.
Arguments:
- adjoint_init: bfloat16 [8, 9, 16, 128, 128], P('event', None, None, 'lon'), may hold values from -6 to 6
- forward_state: bfloat16 [8, 8, 9, 16, 128, 128], P('event', None, None, None, 'lon'), may hold values from -3 to 3
- p_speed: float32 [16, 128, 128], P(None, 'lon'), may hold values from 0.3 to 0.5
- s_speed: float32 [16, 128, 128], P(None, 'lon'), may hold values from 0.1 to 0.2
- density: float32 [16, 128, 128], P(None, 'lon'), may hold values from 0.8 to 1.6
Outputs:
- kernels: float32 [3, 16, 128, 128], P(None, 'event', 'lon')
All inputs are finite; a program needn't handle non-finite values.
Results may differ from a plain program's by a relative error of at most 0.015.
Values may be sent and summed in bfloat16 or wider, within the bound.
A program may use at most 64 MiB of HBM per device.

v0:
```python
import jax
import jax.numpy as jnp
from jax import lax
from jax.sharding import PartitionSpec as P


def with_halo(value, sides, width):
    for axis, dim in sides:
        devices, length = (lax.axis_size(axis), value.shape[dim])
        up = [(i, (i + 1) % devices) for i in range(devices)]
        down = [(j, i) for i, j in up]
        last = lax.slice_in_dim(value, length - width, length, axis=dim)
        initial = lax.slice_in_dim(value, 0, width, axis=dim)
        before = lax.ppermute(last, axis, up)
        after = lax.ppermute(initial, axis, down)
        value = jnp.concatenate([before, value, after], axis=dim)
    return value


def ahead_diff(values, along):
    length = values.shape[along]
    border = jnp.zeros_like(lax.slice_in_dim(values, 0, 1, axis=along))
    return (
        jnp.concatenate([lax.slice_in_dim(values, 1, length, axis=along), border], axis=along)
        - values
    )


def behind_diff(values, along):
    length = values.shape[along]
    border = jnp.zeros_like(lax.slice_in_dim(values, 0, 1, axis=along))
    return values - jnp.concatenate(
        [border, lax.slice_in_dim(values, 0, length - 1, axis=along)], axis=along
    )


def forcing(stress):
    stress_xx, stress_yy, stress_zz, stress_xy, stress_xz, stress_yz = [
        stress[index].astype(jnp.float32) for index in range(6)
    ]
    force_x = ahead_diff(stress_xx, 1) + behind_diff(stress_xy, 2) + behind_diff(stress_xz, 0)
    force_y = behind_diff(stress_xy, 1) + ahead_diff(stress_yy, 2) + behind_diff(stress_yz, 0)
    force_z = behind_diff(stress_xz, 1) + behind_diff(stress_yz, 2) + ahead_diff(stress_zz, 0)
    return (force_x, force_y, force_z)


def strain_rates(velocity):
    speed_x, speed_y, speed_z = [velocity[index].astype(jnp.float32) for index in range(3)]
    rate_xx = behind_diff(speed_x, 1)
    rate_yy = behind_diff(speed_y, 2)
    rate_zz = behind_diff(speed_z, 0)
    rate_xy = 0.5 * (ahead_diff(speed_x, 2) + ahead_diff(speed_y, 1))
    rate_xz = 0.5 * (ahead_diff(speed_x, 0) + ahead_diff(speed_z, 1))
    rate_yz = 0.5 * (ahead_diff(speed_y, 0) + ahead_diff(speed_z, 2))
    return (rate_xx, rate_yy, rate_zz, rate_xy, rate_xz, rate_yz)


def update_stress(stress, strain_rate, lame_coef, shear_coef):
    rate_xx, rate_yy, rate_zz, rate_xy, rate_xz, rate_yz = strain_rate
    trace_rate = rate_xx + rate_yy + rate_zz
    twice_shear = 2.0 * shear_coef
    volume_part = lame_coef * trace_rate
    updated = [
        stress[0].astype(jnp.float32) + volume_part + twice_shear * rate_xx,
        stress[1].astype(jnp.float32) + volume_part + twice_shear * rate_yy,
        stress[2].astype(jnp.float32) + volume_part + twice_shear * rate_zz,
        stress[3].astype(jnp.float32) + twice_shear * rate_xy,
        stress[4].astype(jnp.float32) + twice_shear * rate_xz,
        stress[5].astype(jnp.float32) + twice_shear * rate_yz,
    ]
    return jnp.stack([item.astype(jnp.bfloat16) for item in updated])


def kernel_terms(velocity, strain_rate, forward_now):
    rate_xx, rate_yy, rate_zz, rate_xy, rate_xz, rate_yz = strain_rate
    forward_f = [forward_now[index].astype(jnp.float32) for index in range(9)]
    trace_rate = rate_xx + rate_yy + rate_zz
    lame_term = trace_rate * (forward_f[3] + forward_f[4] + forward_f[5])
    shear_term = 2.0 * (
        rate_xx * forward_f[3]
        + rate_yy * forward_f[4]
        + rate_zz * forward_f[5]
        + 2.0 * (rate_xy * forward_f[6] + rate_xz * forward_f[7] + rate_yz * forward_f[8])
    )
    speed = [velocity[index].astype(jnp.float32) for index in range(3)]
    density_term = speed[0] * forward_f[0] + speed[1] * forward_f[1] + speed[2] * forward_f[2]
    return (lame_term, shear_term, density_term)


def combine_kernels(kernel_total, p_speed, s_speed, density):
    lame_coef = density * (p_speed * p_speed - 2.0 * s_speed * s_speed)
    shear_coef = density * s_speed * s_speed
    return jnp.stack(
        [
            2.0 * density * p_speed * p_speed * kernel_total[0],
            2.0 * density * s_speed * s_speed * (kernel_total[1] - 2.0 * kernel_total[0]),
            density * kernel_total[2] + lame_coef * kernel_total[0] + shear_coef * kernel_total[1],
        ]
    )


def settle(kernel_sums, kernel_parts):
    return (kernel_sums, kernel_parts)


def shards(adjoint_init, forward_state, p_speed, s_speed, density):
    fields = adjoint_init[0]
    forward = forward_state[0]
    step_count = forward.shape[0]
    own_width = fields.shape[2]
    kernel_sums = jnp.zeros((3,) + p_speed.shape, jnp.float32)
    kernel_parts = []
    rim_depth = 2 * step_count
    extended = with_halo(fields, (("lon", 2),), rim_depth)
    material = with_halo(jnp.stack([p_speed, s_speed, density]), (("lon", 2),), rim_depth)
    wide_lame = material[2] * (material[0] * material[0] - 2.0 * material[1] * material[1])
    wide_shear = material[2] * material[1] * material[1]
    wide_buoyancy = 1.0 / material[2]
    for step_index in range(step_count):
        force = forcing(extended[3:9])
        velocity = jnp.stack(
            [
                (extended[index].astype(jnp.float32) + wide_buoyancy * force[index]).astype(
                    jnp.bfloat16
                )
                for index in range(3)
            ]
        )
        strain_rate = strain_rates(velocity)
        stress = update_stress(extended[3:9], strain_rate, wide_lame, wide_shear)
        extended = jnp.concatenate([velocity, stress])
        inner_rate = tuple(
            (
                lax.slice_in_dim(item, rim_depth, rim_depth + own_width, axis=1)
                for item in strain_rate
            )
        )
        inner_speed = lax.slice_in_dim(velocity, rim_depth, rim_depth + own_width, axis=2)
        kernel_sums = kernel_sums + jnp.stack(
            kernel_terms(inner_speed, inner_rate, forward[step_index])
        )
        kernel_sums, kernel_parts = settle(kernel_sums, kernel_parts)
    kernel_total = lax.psum_scatter(kernel_sums, "event", scatter_dimension=1, tiled=True)
    row_count = kernel_total.shape[1]
    first_row = lax.axis_index("event") * row_count
    own_rows = [
        lax.dynamic_slice_in_dim(item, first_row, row_count, 0)
        for item in (p_speed, s_speed, density)
    ]
    return combine_kernels(kernel_total, own_rows[0], own_rows[1], own_rows[2])


def solution(mesh):
    placed = (
        P("event", None, None, "lon", None),
        P("event", None, None, None, "lon", None),
        P(None, "lon", None),
        P(None, "lon", None),
        P(None, "lon", None),
    )
    return jax.shard_map(
        shards, mesh=mesh, in_specs=placed, out_specs=P(None, "event", "lon", None), check_vma=False
    )
```

profile of v0, /device:TPU:0, one launch (start us, length us, event | category | flops | bytes accessed | tf_op | source)
XLA Modules:
  0.0 168.5 jit_solution(11118368824042355174)
XLA Ops:
  6.5 1.5 fusion.169
  8.6 2.0 %collective-permute-start.1 = (bf16[9,16,16,128]{3,2,1,0:T(8,128)(2,1)S(1)}, bf16[9,16,16,128]{3,2,1,0:T(8,128)(2,1)S(1)}, u32[]{:S(2)}, u32[]{:S(2)}) collective-permute-start(bf16[9,16,16,128]{3,2,1,0:T(8,128)(2,1)S(1)} %get-tuple-element.152), channel_id=1, source_target_pairs={{1,0},{2,1},{3,2},{0,3},{5,4},{6,5},{7,6},{4,7},{9,8},{10,9},{11,1... | collective-permute-start | bytes 1769480 | tf_op jit(solution)/shard_map/ppermute | solution.py:15
  11.4 1.1 collective-permute-start.3
  12.6 17.7 %collective-permute-done.2 = f32[3,16,16,128]{3,2,1,0:T(8,128)S(1)} collective-permute-done((f32[3,16,16,128]{3,2,1,0:T(8,128)S(1)}, f32[3,16,16,128]{3,2,1,0:T(8,128)S(1)}, u32[]{:S(2)}, u32[]{:S(2)}) %collective-permute-start.2) | collective-permute-done | bytes 393248 | tf_op jit(solution)/shard_map/ppermute | solution.py:14
  30.3 2.4 %collective-permute-done.3 = f32[3,16,16,128]{3,2,1,0:T(8,128)S(1)} collective-permute-done((f32[3,16,16,128]{3,2,1,0:T(8,128)S(1)}, f32[3,16,16,128]{3,2,1,0:T(8,128)S(1)}, u32[]{:S(2)}, u32[]{:S(2)}) %collective-permute-start.3) | collective-permute-done | bytes 393248 | tf_op jit(solution)/shard_map/ppermute | solution.py:15
  32.9 0.7 pad_maximum_fusion
  34.2 0.7 fusion.12
  36.1 1.4 fusion.74
  37.6 1.9 %fusion.75 = (f32[16,64,128]{2,1,0:T(8,128)S(1)}, f32[16,64,128]{2,1,0:T(8,128)S(1)}, bf16[16,64,128]{2,1,0:T(8,128)(2,1)S(1)}, f32[16,64,128]{2,1,0:T(8,128)}, ...) fusion(f32[16,64,128]{2,1,0:T(8,128)S(1)} %get-tuple-element.80, ...), kind=kLoop, calls=%fused_computation.243 | loop fusion | flops 5111808 | bytes 10657792 | tf_op jit(solution)/shard_map/convert_element_type | solution.py:39
  40.8 0.7 add_convert_fusion.58
  41.9 1.2 fusion.76
  43.9 0.7 add_convert_fusion.50
  45.9 2.2 %fusion.79 = (f32[16,64,128]{2,1,0:T(8,128)S(1)}, f32[16,64,128]{2,1,0:T(8,128)S(1)}, f32[16,64,128]{2,1,0:T(8,128)S(1)}, f32[16,64,128]{2,1,0:T(8,128)S(1)}, f3...) fusion(f32[16,64,128]{2,1,0:T(8,128)S(1)} %get-tuple-element.80, ...), kind=kLoop, calls=%fused_computation.247 | loop fusion | flops 4980736 | bytes 12709888 | tf_op jit(solution)/shard_map/convert_element_type | solution.py:39
  48.9 0.9 add_convert_fusion.41
  51.0 2.3 %fusion.82 = (f32[16,64,128]{2,1,0:T(8,128)S(1)}, f32[16,64,128]{2,1,0:T(8,128)S(1)}, f32[16,64,128]{2,1,0:T(8,128)}, f32[16,64,128]{2,1,0:T(8,128)S(1)}, f32[16...) fusion(f32[16,64,128]{2,1,0:T(8,128)S(1)} %get-tuple-element.80, ...), kind=kLoop, calls=%fused_computation.250 | loop fusion | flops 4980736 | bytes 12709888 | tf_op jit(solution)/shard_map/convert_element_type | solution.py:39
  54.1 0.7 add_convert_fusion.32
  56.1 2.4 %fusion.85 = (f32[16,64,128]{2,1,0:T(8,128)S(1)}, f32[16,64,128]{2,1,0:T(8,128)S(1)}, f32[16,64,128]{2,1,0:T(8,128)}, f32[16,64,128]{2,1,0:T(8,128)S(1)}, f32[16...) fusion(f32[16,64,128]{2,1,0:T(8,128)S(1)} %get-tuple-element.80, ...), kind=kLoop, calls=%fused_computation.253 | loop fusion | flops 4980736 | bytes 12709888 | tf_op jit(solution)/shard_map/convert_element_type | solution.py:39
  61.2 2.3 %fusion.88 = (f32[16,64,128]{2,1,0:T(8,128)S(1)}, f32[16,64,128]{2,1,0:T(8,128)S(1)}, f32[16,64,128]{2,1,0:T(8,128)}, f32[16,64,128]{2,1,0:T(8,128)S(1)}, f32[16...) fusion(f32[16,64,128]{2,1,0:T(8,128)S(1)} %get-tuple-element.80, ...), kind=kLoop, calls=%fused_computation.256 | loop fusion | flops 4980736 | bytes 12709888 | tf_op jit(solution)/shard_map/convert_element_type | solution.py:39
  66.5 2.6 %fusion.91 = (f32[16,64,128]{2,1,0:T(8,128)S(1)}, f32[16,64,128]{2,1,0:T(8,128)S(1)}, f32[16,64,128]{2,1,0:T(8,128)}, f32[16,64,128]{2,1,0:T(8,128)S(1)}, f32[16...) fusion(f32[16,64,128]{2,1,0:T(8,128)S(1)} %get-tuple-element.80, ...), kind=kLoop, calls=%fused_computation.259 | loop fusion | flops 5373952 | bytes 13496320 | tf_op jit(solution)/shard_map/convert_element_type | solution.py:39
  70.6 0.9 fusion.164
  71.9 1.3 slice-done.1
  81.5 1.7 fusion.5
  84.5 75.7 %all-reduce.147.cloned.1.call-done = f32[3,16,32,128]{3,2,1,0:T(8,128)} async-done(((f32[3,16,32,128]{3,2,1,0:T(8,128)}), f32[3,16,32,128]{3,2,1,0:T(8,128)}) %all-reduce.147.cloned.1.call-update) | async-done | bytes 786448
  160.2 0.8 fusion.153
  (237 shorter events, 27.1 us)
Async XLA Ops:
  6.5 4.1 %copy-start.2 = (f32[16,32,128]{2,1,0:T(8,128)S(1)}, f32[16,32,128]{2,1,0:T(8,128)}, u32[]{:S(2)}) copy-start(f32[16,32,128]{2,1,0:T(8,128)} %param.9) | copy-start | bytes 786436
  6.5 4.1 %copy-start.3 = (f32[16,32,128]{2,1,0:T(8,128)S(1)}, f32[16,32,128]{2,1,0:T(8,128)}, u32[]{:S(2)}) copy-start(f32[16,32,128]{2,1,0:T(8,128)} %param.8) | copy-start | bytes 786436
  6.5 4.1 %copy-start.1 = (f32[16,32,128]{2,1,0:T(8,128)S(1)}, f32[16,32,128]{2,1,0:T(8,128)}, u32[]{:S(2)}) copy-start(f32[16,32,128]{2,1,0:T(8,128)} %param.7) | copy-start | bytes 786436
  6.5 153.6 %all-reduce.147.cloned.1.call-start = ((), (), s32[]{:S(2)}) async-start(), calls=%async_computation | async-start | bytes 1572864
  8.1 24.8 %collective-permute-start = (bf16[9,16,16,128]{3,2,1,0:T(8,128)(2,1)S(1)}, bf16[9,16,16,128]{3,2,1,0:T(8,128)(2,1)S(1)}, u32[]{:S(2)}, u32[]{:S(2)}) collective-permute-start(bf16[9,16,16,128]{3,2,1,0:T(8,128)(2,1)S(1)} %get-tuple-element.151), channel_id=1, source_target_pairs={{0,1},{1,2},{2,3},{3,0},{4,5},{5,6},{6,7},{7,4},{8,9},{9,10},{10,1... | collective-permute-start | bytes 1769480 | tf_op jit(solution)/shard_map/ppermute | solution.py:14
  8.6 24.3 %collective-permute-start.1 = (bf16[9,16,16,128]{3,2,1,0:T(8,128)(2,1)S(1)}, bf16[9,16,16,128]{3,2,1,0:T(8,128)(2,1)S(1)}, u32[]{:S(2)}, u32[]{:S(2)}) collective-permute-start(bf16[9,16,16,128]{3,2,1,0:T(8,128)(2,1)S(1)} %get-tuple-element.152), channel_id=1, source_target_pairs={{1,0},{2,1},{3,2},{0,3},{5,4},{6,5},{7,6},{4,7},{9,8},{10,9},{11,1... | collective-permute-start | bytes 1769480 | tf_op jit(solution)/shard_map/ppermute | solution.py:15
  10.8 19.5 %collective-permute-start.2 = (f32[3,16,16,128]{3,2,1,0:T(8,128)S(1)}, f32[3,16,16,128]{3,2,1,0:T(8,128)S(1)}, u32[]{:S(2)}, u32[]{:S(2)}) collective-permute-start(f32[3,16,16,128]{3,2,1,0:T(8,128)S(1)} %get-tuple-element.201), channel_id=1, source_target_pairs={{0,1},{1,2},{2,3},{3,0},{4,5},{5,6},{6,7},{7,4},{8,9},{9,10},{10,1... | collective-permute-start | bytes 1179656 | tf_op jit(solution)/shard_map/ppermute | solution.py:14
  11.4 21.4 %copy-start = (bf16[1,9,16,32,128]{4,3,2,1,0:T(8,128)(2,1)S(1)}, bf16[1,9,16,32,128]{4,3,2,1,0:T(8,128)(2,1)}, u32[]{:S(2)}) copy-start(bf16[1,9,16,32,128]{4,3,2,1,0:T(8,128)(2,1)} %param.5) | copy-start | bytes 3538948
  11.4 21.2 %collective-permute-start.3 = (f32[3,16,16,128]{3,2,1,0:T(8,128)S(1)}, f32[3,16,16,128]{3,2,1,0:T(8,128)S(1)}, u32[]{:S(2)}, u32[]{:S(2)}) collective-permute-start(f32[3,16,16,128]{3,2,1,0:T(8,128)S(1)} %get-tuple-element.202), channel_id=1, source_target_pairs={{1,0},{2,1},{3,2},{0,3},{5,4},{6,5},{7,6},{4,7},{9,8},{10,9},{11,1... | collective-permute-start | bytes 1179656 | tf_op jit(solution)/shard_map/ppermute | solution.py:15
  69.6 2.4 %slice-start = ((s8[9437184]{0:T(1024)(128)(4,1)}), s8[4194304]{0:T(1024)(128)(4,1)S(1)}, s32[]{:S(2)}) async-start(s8[9437184]{0:T(1024)(128)(4,1)} %bitcast.522), calls=%async_computation.1 | async-start | bytes 8388608
  70.3 2.9 %slice-start.1 = ((s8[9437184]{0:T(1024)(128)(4,1)}), s8[4194304]{0:T(1024)(128)(4,1)S(1)}, s32[]{:S(2)}) async-start(s8[9437184]{0:T(1024)(128)(4,1)} %bitcast.522), calls=%async_computation.2 | async-start | bytes 8388608
  70.6 2.9 %slice-start.2 = ((s8[9437184]{0:T(1024)(128)(4,1)}), s8[1048576]{0:T(1024)(128)(4,1)S(1)}, s32[]{:S(2)}) async-start(s8[9437184]{0:T(1024)(128)(4,1)} %bitcast.522), calls=%async_computation.3 | async-start | bytes 2097152
  71.7 1.8 %copy-start.23 = (f32[16,64,128]{2,1,0:T(8,128)S(1)}, f32[16,64,128]{2,1,0:T(8,128)}, u32[]{:S(2)}) copy-start(f32[16,64,128]{2,1,0:T(8,128)} %get-tuple-element.81) | copy-start | bytes 1572868
  71.7 1.9 %copy-start.24 = (f32[16,64,128]{2,1,0:T(8,128)S(1)}, f32[16,64,128]{2,1,0:T(8,128)}, u32[]{:S(2)}) copy-start(f32[16,64,128]{2,1,0:T(8,128)} %get-tuple-element.121) | copy-start | bytes 1572868
  71.7 2.1 %copy-start.25 = (f32[16,64,128]{2,1,0:T(8,128)S(1)}, f32[16,64,128]{2,1,0:T(8,128)}, u32[]{:S(2)}) copy-start(f32[16,64,128]{2,1,0:T(8,128)} %get-tuple-element.123) | copy-start | bytes 1572868
  71.8 2.2 %copy-start.26 = (f32[16,64,128]{2,1,0:T(8,128)S(1)}, f32[16,64,128]{2,1,0:T(8,128)}, u32[]{:S(2)}) copy-start(f32[16,64,128]{2,1,0:T(8,128)} %get-tuple-element.125) | copy-start | bytes 1572868
  74.6 1.6 copy-start.9
  74.6 1.7 %copy-start.10 = (f32[16,64,128]{2,1,0:T(8,128)S(1)}, f32[16,64,128]{2,1,0:T(8,128)}, u32[]{:S(2)}) copy-start(f32[16,64,128]{2,1,0:T(8,128)} %get-tuple-element.184) | copy-start | bytes 1572868
  75.9 1.6 copy-start.14
  76.6 1.5 copy-start.17
  76.6 1.6 copy-start.18
  77.8 1.5 copy-start.21
  77.8 1.6 copy-start.22
  81.5 1.7 %copy-start.27 = (u32[32]{0:T(128)S(1)}, u32[32]{0:T(128)}, u32[]{:S(2)}) copy-start(u32[32]{0:T(128)} %constant.316) | copy-start | bytes 388
  (12 other events, 15.3 us)
Sparse Core Ops, SparseCore 0:
  83.3 76.7 all-reduce.146
where the time goes:
time: 169 us; the launch traced here: 168 us
  waiting for transfers between devices  95.9 us (57%)
  other arithmetic  36 us (21%)
  local copies, waits for them, and re-layouts  16.7 us (10%)
  between operations  15.5 us (9%)
  starting transfers between devices  4.35 us (3%)
    unnamed x2, waiting for transfers between devices  75.7 us
    convert_element_type x15, other arithmetic, forcing(): stress[index].astype(jnp.float32)  18.6 us
    ppermute x2, waiting for transfers between devices, with_halo(): before = lax.ppermute(last, axis, up)  17.7 us
    convert_element_type x14, other arithmetic, shards(): (extended[index].astype(jnp.float32) + wide_buoyancy * force[index]).asty...  8.2 us
    slice x72, local copies, waits for them, and re-layouts, ahead_diff(): lax.slice_in_dim(values, 1, length, axis=along)  6.35 us
    unnamed x63, local copies, waits for them, and re-layouts  6.21 us
  transfers between devices with their start and end apart: 5, of which 3 were waited for; matrix products, arithmetic and copies ran while one was open for 1% of the time, Pallas kernels for 0%

commit v1 on v0

v1 whole, which is shorter than its diff:
```python
import functools

import jax
import jax.numpy as jnp
from jax import lax
from jax.experimental import pallas as pl
from jax.experimental.pallas import tpu as pltpu
from jax.sharding import PartitionSpec as P

VX, VY, VZ, XX, YY, ZZ, XY, XZ, YZ = range(9)
HALO = 4
TILE = 8
PAD = 8
UNROLL = 2


def behind_lat(a):
    lane = lax.broadcasted_iota(jnp.int32, a.shape, 1)
    return a - jnp.where(lane == 0, 0.0, pltpu.roll(a, 1, 1))


def ahead_lat(a):
    lane = lax.broadcasted_iota(jnp.int32, a.shape, 1)
    last = a.shape[1] - 1
    return jnp.where(lane == last, 0.0, pltpu.roll(a, last, 1)) - a


def kernel(
    adj_hbm, fwd_hbm, p_hbm, s_hbm, d_hbm, out_ref,
    adj, fwd, p_raw, s_raw, d_raw, w, mat, acc,
    first_out, first_in, next_out, next_in, red_out, red_in,
    local_sem, fwd_sem, halo_send, halo_recv, red_send, red_recv,
):
    levels, own, lat = p_raw.shape
    steps = fwd.shape[0]
    events, ring = lax.axis_size("event"), lax.axis_size("lon")
    me_e, me_l = lax.axis_index("event"), lax.axis_index("lon")
    right, left = lax.rem(me_l + 1, ring), lax.rem(me_l + ring - 1, ring)
    share = levels // events

    local = [
        pltpu.make_async_copy(src, dst, local_sem.at[i])
        for i, (src, dst) in enumerate(
            ((adj_hbm.at[0], adj), (d_hbm, d_raw), (p_hbm, p_raw), (s_hbm, s_raw))
        )
    ]
    for copy in local:
        copy.start()

    def fwd_copy(t):
        return pltpu.make_async_copy(fwd_hbm.at[0, t], fwd.at[t], fwd_sem.at[t])

    for t in range(steps):
        fwd_copy(t).start()

    barrier = pltpu.get_barrier_semaphore()
    for neighbour in (left, right):
        pl.semaphore_signal(
            barrier, inc=1, device_id=(me_e, neighbour), device_id_type=pl.DeviceIdType.MESH
        )
    for d in range(1, events):
        pl.semaphore_signal(
            barrier, inc=1, device_id=(lax.rem(me_e + d, events), me_l),
            device_id_type=pl.DeviceIdType.MESH,
        )

    zeros = jnp.zeros((w.shape[2], lat), jnp.float32)
    for f in (XZ, YZ, VZ):
        w[f, 0] = zeros
    for f in (ZZ, VX, VY):
        w[f, levels + 1] = zeros

    upper = lax.broadcasted_iota(jnp.int32, (TILE, lat), 0) < HALO

    def pack(get, put):
        def edges(j):
            a, b = get(j, 0), get(j + 1, 0)
            c, d = get(j, own - TILE), get(j + 1, own - TILE)
            return (
                jnp.where(upper, a, pltpu.roll(b, HALO, 0)),
                jnp.where(upper, pltpu.roll(c, HALO, 0), d),
            )

        lo, hi = edges(0), edges(2)
        for side in range(2):
            put(side, jnp.concatenate([lo[side], hi[side]], axis=0).astype(jnp.bfloat16))

    def unpack(from_right, from_left, put):
        r16, l16 = from_right.astype(jnp.float32), from_left.astype(jnp.float32)
        for half in range(2):
            r, l = (v[half * TILE:(half + 1) * TILE] for v in (r16, l16))
            put(2 * half, jnp.where(upper, r, pltpu.roll(l, HALO, 0)))
            put(2 * half + 1, jnp.where(upper, pltpu.roll(r, HALO, 0), l))

    quads = levels // 4
    local[0].wait()

    def load_fields(q, carry):
        for f in range(9):
            for j in range(4):
                rows = adj[f, q * 4 + j].astype(jnp.float32)
                w[f, q * 4 + j + 1, PAD:PAD + own, :] = rows
                if f == XX:
                    w[f, q * 4 + j + 1, PAD + own + TILE:PAD + own + 2 * TILE, :] = rows[:TILE]
        return carry

    lax.fori_loop(0, quads, load_fields, 0)

    for copy in local[1:]:
        copy.wait()

    def load_material(z, carry):
        d, p, s = d_raw[z], p_raw[z], s_raw[z]
        mat[0, z, 0:own, :] = 1.0 / d
        mat[1, z, 0:own, :] = d * (p * p - 2.0 * s * s)
        mat[2, z, 0:own, :] = d * s * s
        return carry

    lax.fori_loop(0, levels, load_material, 0)

    def pack_fields(out):
        def body(q, carry):
            for f in range(9):
                def put(side, value, f=f):
                    out[side, f, q] = value

                pack(lambda j, r, f=f: w[f, q * 4 + j + 1, PAD + r:PAD + r + TILE, :], put)
            return carry

        lax.fori_loop(0, quads, body, 0)

    def pack_material(q, carry):
        for f in range(3):
            def put(side, value, f=f):
                first_out[side, 9 + f, q] = value

            pack(lambda j, r, f=f: mat[f, q * 4 + j, r:r + TILE, :], put)
        return carry

    pack_fields(first_out)
    lax.fori_loop(0, quads, pack_material, 0)
    pl.semaphore_wait(barrier, events + 1)

    def exchange(src, dst, at):
        return [
            pltpu.make_async_remote_copy(
                src_ref=src.at[side], dst_ref=dst.at[side],
                send_sem=halo_send.at[at, side], recv_sem=halo_recv.at[at, side],
                device_id=(me_e, target), device_id_type=pl.DeviceIdType.MESH,
            )
            for side, target in ((0, left), (1, right))
        ]

    def unpack_fields(src):
        def body(q, carry):
            for f in range(9):
                def put(j, tile, f=f):
                    w[f, q * 4 + j + 1, PAD + own:PAD + own + TILE, :] = tile
                    if f in (XY, XZ):
                        w[f, q * 4 + j + 1, 0:TILE, :] = tile

                unpack(src[0, f, q], src[1, f, q], put)
            return carry

        lax.fori_loop(0, quads, body, 0)

    blocks = [(r, 2 * TILE) for r in range(0, own, 2 * TILE)] + [(own, TILE)]

    def velocity_level(z):
        for r, n in blocks:
            def ld(f, off=0, dz=0):
                return w[f, z + 1 + dz, pl.ds(PAD + r + off, n), :]

            buoy = mat[0, z, r:r + n, :]
            xy, xz, yz, zz = ld(XY), ld(XZ), ld(YZ), ld(ZZ)
            fx = (ld(XX, 1) - ld(XX)) + behind_lat(xy) + (xz - ld(XZ, 0, -1))
            fy = (xy - ld(XY, -1)) + ahead_lat(ld(YY)) + (yz - ld(YZ, 0, -1))
            fz = (xz - ld(XZ, -1)) + behind_lat(yz) + (ld(ZZ, 0, 1) - zz)
            for f, force in ((VX, fx), (VY, fy), (VZ, fz)):
                v = ld(f) + buoy * force
                w[f, z + 1, PAD + r:PAD + r + n, :] = v
                if r == 0 and f in (VY, VZ):
                    w[f, z + 1, PAD + own + TILE:PAD + own + 2 * TILE, :] = v[:TILE]
                if r == own and f == VX:
                    w[f, z + 1, 0:TILE, :] = v

    def rates(z, r, n):
        def ld(f, off=0, dz=0):
            return w[f, z + 1 + dz, pl.ds(PAD + r + off, n), :]

        vx, vy, vz = ld(VX), ld(VY), ld(VZ)
        exx = vx - ld(VX, -1)
        eyy = behind_lat(vy)
        ezz = vz - ld(VZ, 0, -1)
        gxy = ahead_lat(vx) + (ld(VY, 1) - vy)
        gxz = (ld(VX, 0, 1) - vx) + (ld(VZ, 1) - vz)
        gyz = (ld(VY, 0, 1) - vy) + ahead_lat(vz)
        return (vx, vy, vz), (exx, eyy, ezz, gxy, gxz, gyz), exx + eyy + ezz

    def terms(t, z, r, n, v, e, tr):
        F = [fwd[t, f, z, r:r + n, :].astype(jnp.float32) for f in range(9)]
        k_lame = tr * (F[3] + F[4] + F[5])
        half_shear = (e[0] * F[3] + e[1] * F[4] + e[2] * F[5]) + (
            e[3] * F[6] + e[4] * F[7] + e[5] * F[8]
        )
        k_dens = v[0] * F[0] + v[1] * F[1] + v[2] * F[2]
        return k_lame, half_shear, k_dens

    def stress_level(t, z):
        for r, n in blocks:
            v, e, tr = rates(z, r, n)
            lame, shear = mat[1, z, r:r + n, :], mat[2, z, r:r + n, :]
            volume, twice = lame * tr, shear + shear
            for i, f in enumerate((XX, YY, ZZ, XY, XZ, YZ)):
                rows = slice(PAD + r, PAD + r + n)
                s = w[f, z + 1, rows, :]
                s = (s + volume) + twice * e[i] if i < 3 else s + shear * e[i]
                w[f, z + 1, rows, :] = s
                if r == 0 and f == XX:
                    w[f, z + 1, PAD + own + TILE:PAD + own + 2 * TILE, :] = s[:TILE]
                if r == own and f in (XY, XZ):
                    w[f, z + 1, 0:TILE, :] = s
            if r < own:
                for i, term in enumerate(terms(t, z, r, n, v, e, tr)):
                    acc[i, z, r:r + n, :] += term

    def sweep(level):
        def body(i, carry):
            for j in range(UNROLL):
                level(i * UNROLL + j)
            return carry

        lax.fori_loop(0, levels // UNROLL, body, 0)

    def step(t, carry):
        sweep(velocity_level)
        fwd_copy(t).wait()
        sweep(functools.partial(stress_level, t))
        return carry

    def clear(z, carry):
        for i in range(3):
            acc[i, z] = jnp.zeros((own, lat), jnp.float32)
        return carry

    copies = exchange(first_out, first_in, 0)
    for copy in copies:
        copy.start()
    lax.fori_loop(0, levels, clear, 0)
    for copy in copies:
        copy.wait()
    unpack_fields(first_in)

    def unpack_material(q, carry):
        for f in range(3):
            def put(j, tile, f=f):
                mat[f, q * 4 + j, own:own + TILE, :] = tile

            unpack(first_in[0, 9 + f, q], first_in[1, 9 + f, q], put)
        return carry

    lax.fori_loop(0, quads, unpack_material, 0)

    for epoch in range(-(-steps // HALO)):
        if epoch:
            pack_fields(next_out.at[epoch - 1])
            copies = exchange(next_out.at[epoch - 1], next_in.at[epoch - 1], epoch)
            for copy in copies:
                copy.start()
            for copy in copies:
                copy.wait()
            unpack_fields(next_in.at[epoch - 1])
        lax.fori_loop(epoch * HALO, min((epoch + 1) * HALO, steps - 1), step, 0)

    sweep(velocity_level)
    last = steps - 1
    fwd_copy(last).wait()

    def last_levels(owner, write):
        for j in range(share):
            z = owner * share + j
            for r, n in blocks[:-1]:
                v, e, tr = rates(z, r, n)
                for i, term in enumerate(terms(last, z, r, n, v, e, tr)):
                    write(i, j, z, r, n, acc[i, z, r:r + n, :] + term)

    def red_copy(d, owner):
        return pltpu.make_async_remote_copy(
            src_ref=red_out.at[d], dst_ref=red_in.at[d],
            send_sem=red_send.at[d], recv_sem=red_recv.at[d],
            device_id=(owner, me_l), device_id_type=pl.DeviceIdType.MESH,
        )

    def send_levels(d, carry):
        owner = lax.rem(me_e + d + 1, events)

        def write(i, j, z, r, n, total):
            red_out[d, i, j, r:r + n, :] = total.astype(jnp.bfloat16)

        last_levels(owner, write)
        red_copy(d, owner).start()
        return carry

    lax.fori_loop(0, events - 1, send_levels, 0)

    def keep(i, j, z, r, n, total):
        acc[i, z, r:r + n, :] = total

    last_levels(me_e, keep)

    def finish_copies(d, carry):
        red_copy(d, lax.rem(me_e + d + 1, events)).wait()
        return carry

    lax.fori_loop(0, events - 1, finish_copies, 0)

    for j in range(share):
        z = me_e * share + j
        for r, n in blocks[:-1]:
            k_lame, half_shear, k_dens = (
                acc[i, z, r:r + n, :]
                + sum(red_in[d, i, j, r:r + n, :].astype(jnp.float32) for d in range(events - 1))
                for i in range(3)
            )
            k_shear = 2.0 * half_shear
            p, s, d = (x[z, r:r + n, :] for x in (p_raw, s_raw, d_raw))
            lame, shear = d * (p * p - 2.0 * s * s), d * s * s
            out_ref[0, j, r:r + n, :] = 2.0 * d * p * p * k_lame
            out_ref[1, j, r:r + n, :] = 2.0 * d * s * s * (k_shear - 2.0 * k_lame)
            out_ref[2, j, r:r + n, :] = d * k_dens + lame * k_lame + shear * k_shear


def shards(adjoint_init, forward_state, p_speed, s_speed, density):
    levels, own, lat = p_speed.shape
    steps = forward_state.shape[1]
    events = lax.axis_size("event")
    share, quads = levels // events, levels // 4
    epochs = -(-steps // HALO)
    f32, bf16 = jnp.float32, jnp.bfloat16
    anywhere = pl.BlockSpec(memory_space=pl.ANY)
    return pl.pallas_call(
        kernel,
        out_shape=jax.ShapeDtypeStruct((3, share, own, lat), f32),
        in_specs=[anywhere] * 5,
        out_specs=pl.BlockSpec(memory_space=pltpu.VMEM),
        scratch_shapes=[
            pltpu.VMEM(adjoint_init.shape[1:], bf16),
            pltpu.VMEM(forward_state.shape[1:], bf16),
            pltpu.VMEM(p_speed.shape, f32),
            pltpu.VMEM(p_speed.shape, f32),
            pltpu.VMEM(p_speed.shape, f32),
            pltpu.VMEM((9, levels + 2, PAD + own + 2 * TILE, lat), f32),
            pltpu.VMEM((3, levels, own + TILE, lat), f32),
            pltpu.VMEM((3, levels, own, lat), f32),
            pltpu.VMEM((2, 12, quads, 2 * TILE, lat), bf16),
            pltpu.VMEM((2, 12, quads, 2 * TILE, lat), bf16),
            pltpu.VMEM((max(epochs - 1, 1), 2, 9, quads, 2 * TILE, lat), bf16),
            pltpu.VMEM((max(epochs - 1, 1), 2, 9, quads, 2 * TILE, lat), bf16),
            pltpu.VMEM((events - 1, 3, share, own, lat), bf16),
            pltpu.VMEM((events - 1, 3, share, own, lat), bf16),
            pltpu.SemaphoreType.DMA((4,)),
            pltpu.SemaphoreType.DMA((steps,)),
            pltpu.SemaphoreType.DMA((epochs, 2)),
            pltpu.SemaphoreType.DMA((epochs, 2)),
            pltpu.SemaphoreType.DMA((events - 1,)),
            pltpu.SemaphoreType.DMA((events - 1,)),
        ],
        compiler_params=pltpu.CompilerParams(
            collective_id=0, has_side_effects=True, vmem_limit_bytes=40 * 2**20
        ),
        name="adjoint",
    )(adjoint_init, forward_state, p_speed, s_speed, density)


def solution(mesh):
    placed = (
        P("event", None, None, "lon", None),
        P("event", None, None, None, "lon", None),
        P(None, "lon", None),
        P(None, "lon", None),
        P(None, "lon", None),
    )
    return jax.shard_map(
        shards, mesh=mesh, in_specs=placed, out_specs=P(None, "event", "lon", None), check_vma=False
    )
```

time: 169 us -> 50.5 us (0.30)
  waiting for transfers between devices: 95.9 us -> 0 us
  Pallas kernels: 0 us -> 41.8 us
  other arithmetic: 36 us -> 0 us
  between operations: 15.5 us -> 0.01 us
  local copies, waits for them, and re-layouts: 16.7 us -> 8.44 us
  starting transfers between devices: 4.35 us -> 0 us
    unnamed x2 -> x0, waiting for transfers between devices: 75.7 us -> none
    pallas_call x0 -> x1, Pallas kernels: none -> 41.8 us  [shards(): pl.pallas_call(kernel, out_shape=jax.ShapeDtypeStruct((3, share, own, lat...]
    convert_element_type x31 -> x0, other arithmetic: 28.2 us -> none  [the longest x15 18.6 us: forcing(): stress[index].astype(jnp.float32)]
    ppermute x4 -> x0, waiting for transfers between devices: 20.1 us -> none  [the longest x2 17.7 us: with_halo(): before = lax.ppermute(last, axis, up)]
    slice x137 -> x0, local copies, waits for them, and re-layouts: 10.5 us -> none  [the longest x72 6.35 us: ahead_diff(): lax.slice_in_dim(values, 1, length, axis=along)]
    ppermute x4 -> x0, starting transfers between devices: 4.35 us -> none  [the longest x2 3.13 us: with_halo(): after = lax.ppermute(initial, axis, down)]
    another operation x12 -> x0, other arithmetic: 4.25 us -> none  [the longest x9 2.73 us: shards(): jnp.stack(kernel_terms(inner_speed, inner_rate, forward[step_index]))]
    add x4 -> x0, other arithmetic: 2.74 us -> none  [the longest x1 1.68 us: shards(): kernel_sums + jnp.stack(kernel_terms(inner_speed, inner_rate, forward[ste...]
  transfers between devices with their start and end apart: 5 -> 0, of which waited for: 3 -> 0; matrix products, arithmetic and copies ran while one was open for 1% -> 0% of each run, Pallas kernels for 0% -> 0%
where the time goes in v1:
time: 50.5 us; the launch traced here: 50.3 us
  Pallas kernels  41.8 us (83%)
  local copies, waits for them, and re-layouts  8.44 us (17%)
    pallas_call x1, Pallas kernels, shards(): pl.pallas_call(kernel, out_shape=jax.ShapeDtypeStruct((3, share, own, lat...  41.8 us
    unnamed x11, local copies, waits for them, and re-layouts  8.44 us

profile of v1, /device:TPU:0, one launch (start us, length us, event | category | flops | bytes accessed | tf_op | source)
XLA Modules:
  0.0 50.3 jit_solution(4429806612266337587)
XLA Ops:
  0.0 0.0 copy-start
  0.0 3.7 %copy-done = bf16[1,8,9,16,32,128]{5,4,3,2,1,0:T(8,128)(2,1)S(1)} copy-done((bf16[1,8,9,16,32,128]{5,4,3,2,1,0:T(8,128)(2,1)S(1)}, bf16[1,8,9,16,32,128]{5,4,3,2,1,0:T(8,128)(2,1)}, u32[]{:S(2)}) %copy-start) | copy-done | bytes 9437208
  3.7 0.0 copy-start.1
  3.7 1.3 %copy-done.1 = bf16[1,9,16,32,128]{4,3,2,1,0:T(8,128)(2,1)S(1)} copy-done((bf16[1,9,16,32,128]{4,3,2,1,0:T(8,128)(2,1)S(1)}, bf16[1,9,16,32,128]{4,3,2,1,0:T(8,128)(2,1)}, u32[]{:S(2)}) %copy-start.1) | copy-done | bytes 1179672
  5.0 0.0 copy-start.2
  5.0 0.9 %copy-done.2 = f32[16,32,128]{2,1,0:T(8,128)S(1)} copy-done((f32[16,32,128]{2,1,0:T(8,128)S(1)}, f32[16,32,128]{2,1,0:T(8,128)}, u32[]{:S(2)}) %copy-start.2) | copy-done | bytes 262168
  5.9 0.0 copy-start.3
  5.9 0.9 %copy-done.3 = f32[16,32,128]{2,1,0:T(8,128)S(1)} copy-done((f32[16,32,128]{2,1,0:T(8,128)S(1)}, f32[16,32,128]{2,1,0:T(8,128)}, u32[]{:S(2)}) %copy-start.3) | copy-done | bytes 262168
  6.9 0.0 copy-start.4
  6.9 0.9 %copy-done.4 = f32[16,32,128]{2,1,0:T(8,128)S(1)} copy-done((f32[16,32,128]{2,1,0:T(8,128)S(1)}, f32[16,32,128]{2,1,0:T(8,128)}, u32[]{:S(2)}) %copy-start.4) | copy-done | bytes 262168
  7.8 41.8 %adjoint.1 = f32[3,2,32,128]{3,2,1,0:T(8,128)S(1)} custom-call(bf16[1,9,16,32,128]{4,3,2,1,0:T(8,128)(2,1)S(1)} %copy-done.1, bf16[1,8,9,16,32,128]{5,4,3,2,1,0:T(8,128)(2,1)S(1)} %copy-done, f32[16,32,128]{2,1,0:T(8,128)S(1)} %copy-done.2, f32[16,32,128]{2,1,0:T(8,128)S(1)} %copy-done.3, f32[16,32,128]{2,1,0:T(8,128)S(1)} %copy-done.4), custom_call_target="tpu_custom_call" | custom-call | tf_op jit(solution)/shard_map/adjoint/pallas_call | solution.py:341
  49.6 0.6 %copy.7 = f32[3,2,32,128]{3,2,1,0:T(8,128)} copy(f32[3,2,32,128]{3,2,1,0:T(8,128)S(1)} %adjoint.1) | data formatting | bytes 196608
Async XLA Ops:
  0.0 3.7 %copy-start = (bf16[1,8,9,16,32,128]{5,4,3,2,1,0:T(8,128)(2,1)S(1)}, bf16[1,8,9,16,32,128]{5,4,3,2,1,0:T(8,128)(2,1)}, u32[]{:S(2)}) copy-start(bf16[1,8,9,16,32,128]{5,4,3,2,1,0:T(8,128)(2,1)} %fwd_hbm.1) | copy-start | bytes 28311556
  3.7 1.3 %copy-start.1 = (bf16[1,9,16,32,128]{4,3,2,1,0:T(8,128)(2,1)S(1)}, bf16[1,9,16,32,128]{4,3,2,1,0:T(8,128)(2,1)}, u32[]{:S(2)}) copy-start(bf16[1,9,16,32,128]{4,3,2,1,0:T(8,128)(2,1)} %adj_hbm.1) | copy-start | bytes 3538948
  5.0 0.9 %copy-start.2 = (f32[16,32,128]{2,1,0:T(8,128)S(1)}, f32[16,32,128]{2,1,0:T(8,128)}, u32[]{:S(2)}) copy-start(f32[16,32,128]{2,1,0:T(8,128)} %p_hbm.1) | copy-start | bytes 786436
  5.9 0.9 %copy-start.3 = (f32[16,32,128]{2,1,0:T(8,128)S(1)}, f32[16,32,128]{2,1,0:T(8,128)}, u32[]{:S(2)}) copy-start(f32[16,32,128]{2,1,0:T(8,128)} %s_hbm.1) | copy-start | bytes 786436
  6.9 0.9 %copy-start.4 = (f32[16,32,128]{2,1,0:T(8,128)S(1)}, f32[16,32,128]{2,1,0:T(8,128)}, u32[]{:S(2)}) copy-start(f32[16,32,128]{2,1,0:T(8,128)} %d_hbm.1) | copy-start | bytes 786436

commit v2 on v1

--- a/solution.py
+++ b/solution.py
@@ -11,7 +11,7 @@
 HALO = 4
 TILE = 8
 PAD = 8
-UNROLL = 2
+GROUP = 4
 
 
 def behind_lat(a):
@@ -50,9 +50,6 @@
     def fwd_copy(t):
         return pltpu.make_async_copy(fwd_hbm.at[0, t], fwd.at[t], fwd_sem.at[t])
 
-    for t in range(steps):
-        fwd_copy(t).start()
-
     barrier = pltpu.get_barrier_semaphore()
     for neighbour in (left, right):
         pl.semaphore_signal(
@@ -92,77 +89,83 @@
             put(2 * half, jnp.where(upper, r, pltpu.roll(l, HALO, 0)))
             put(2 * half + 1, jnp.where(upper, pltpu.roll(r, HALO, 0), l))
 
-    quads = levels // 4
-    local[0].wait()
-
-    def load_fields(q, carry):
-        for f in range(9):
-            for j in range(4):
-                rows = adj[f, q * 4 + j].astype(jnp.float32)
-                w[f, q * 4 + j + 1, PAD:PAD + own, :] = rows
-                if f == XX:
-                    w[f, q * 4 + j + 1, PAD + own + TILE:PAD + own + 2 * TILE, :] = rows[:TILE]
-        return carry
-
-    lax.fori_loop(0, quads, load_fields, 0)
-
-    for copy in local[1:]:
-        copy.wait()
-
-    def load_material(z, carry):
-        d, p, s = d_raw[z], p_raw[z], s_raw[z]
-        mat[0, z, 0:own, :] = 1.0 / d
-        mat[1, z, 0:own, :] = d * (p * p - 2.0 * s * s)
-        mat[2, z, 0:own, :] = d * s * s
-        return carry
-
-    lax.fori_loop(0, levels, load_material, 0)
-
-    def pack_fields(out):
-        def body(q, carry):
-            for f in range(9):
-                def put(side, value, f=f):
-                    out[side, f, q] = value
-
-                pack(lambda j, r, f=f: w[f, q * 4 + j + 1, PAD + r:PAD + r + TILE, :], put)
-            return carry
-
-        lax.fori_loop(0, quads, body, 0)
-
-    def pack_material(q, carry):
-        for f in range(3):
-            def put(side, value, f=f):
-                first_out[side, 9 + f, q] = value
-
-            pack(lambda j, r, f=f: mat[f, q * 4 + j, r:r + TILE, :], put)
-        return carry
-
-    pack_fields(first_out)
-    lax.fori_loop(0, quads, pack_material, 0)
-    pl.semaphore_wait(barrier, events + 1)
-
-    def exchange(src, dst, at):
+    quads = levels // GROUP
+    flip = jnp.where(me_e * 2 < events, 1, 0)
+
+    def quad_of(i):
+        return i + flip * (quads - 1 - 2 * i)
+
+    def exchange(src, dst, at, i):
         return [
             pltpu.make_async_remote_copy(
-                src_ref=src.at[side], dst_ref=dst.at[side],
-                send_sem=halo_send.at[at, side], recv_sem=halo_recv.at[at, side],
+                src_ref=src.at[i, side], dst_ref=dst.at[i, side],
+                send_sem=halo_send.at[at, i, side], recv_sem=halo_recv.at[at, i, side],
                 device_id=(me_e, target), device_id_type=pl.DeviceIdType.MESH,
             )
             for side, target in ((0, left), (1, right))
         ]
 
-    def unpack_fields(src):
-        def body(q, carry):
+    def pack_fields(out, i, q):
+        for f in range(9):
+            def put(side, value, f=f):
+                out[i, side, f] = value
+
+            pack(lambda j, r, f=f: w[f, q * GROUP + j + 1, PAD + r:PAD + r + TILE, :], put)
+
+    for copy in local:
+        copy.wait()
+    for t in range(steps):
+        fwd_copy(t).start()
+
+    def prepare(i, carry):
+        q = quad_of(i)
+        for j in range(GROUP):
+            z = q * GROUP + j
+            d, p, s = d_raw[z], p_raw[z], s_raw[z]
+            mat[0, z, 0:own, :] = 1.0 / d
+            mat[1, z, 0:own, :] = d * (p * p - 2.0 * s * s)
+            mat[2, z, 0:own, :] = d * s * s
             for f in range(9):
-                def put(j, tile, f=f):
-                    w[f, q * 4 + j + 1, PAD + own:PAD + own + TILE, :] = tile
-                    if f in (XY, XZ):
-                        w[f, q * 4 + j + 1, 0:TILE, :] = tile
-
-                unpack(src[0, f, q], src[1, f, q], put)
-            return carry
-
-        lax.fori_loop(0, quads, body, 0)
+                rows = adj[f, z].astype(jnp.float32)
+                w[f, z + 1, PAD:PAD + own, :] = rows
+                if f == XX:
+                    w[f, z + 1, PAD + own + TILE:PAD + own + 2 * TILE, :] = rows[:TILE]
+        pack_fields(first_out, i, q)
+        for f in range(3):
+            def put(side, value, f=f):
+                first_out[i, side, 9 + f] = value
+
+            pack(lambda j, r, f=f: mat[f, q * GROUP + j, r:r + TILE, :], put)
+
+        @pl.when(i == 0)
+        def _():
+            pl.semaphore_wait(barrier, events + 1)
+
+        for copy in exchange(first_out, first_in, 0, i):
+            copy.start()
+        return carry
+
+    lax.fori_loop(0, quads, prepare, 0)
+
+    def receive(epoch, i):
+        src, dst = (first_out, first_in) if epoch == 0 else (
+            next_out.at[epoch - 1], next_in.at[epoch - 1]
+        )
+        for copy in exchange(src, dst, epoch, i):
+            copy.wait_recv()
+        q = quad_of(i)
+        for f in range(9):
+            def put(j, tile, f=f):
+                w[f, q * GROUP + j + 1, PAD + own:PAD + own + TILE, :] = tile
+                if f in (XY, XZ):
+                    w[f, q * GROUP + j + 1, 0:TILE, :] = tile
+
+            unpack(dst[i, 0, f], dst[i, 1, f], put)
+        for f in range(3 if epoch == 0 else 0):
+            def put_material(j, tile, f=f):
+                mat[f, q * GROUP + j, own:own + TILE, :] = tile
+
+            unpack(dst[i, 0, 9 + f], dst[i, 1, 9 + f], put_material)
 
     blocks = [(r, 2 * TILE) for r in range(0, own, 2 * TILE)] + [(own, TILE)]
 
@@ -224,102 +227,119 @@
                 for i, term in enumerate(terms(t, z, r, n, v, e, tr)):
                     acc[i, z, r:r + n, :] += term
 
-    def sweep(level):
-        def body(i, carry):
-            for j in range(UNROLL):
-                level(i * UNROLL + j)
-            return carry
-
-        lax.fori_loop(0, levels // UNROLL, body, 0)
-
-    def step(t, carry):
-        sweep(velocity_level)
-        fwd_copy(t).wait()
-        sweep(functools.partial(stress_level, t))
-        return carry
-
     def clear(z, carry):
         for i in range(3):
             acc[i, z] = jnp.zeros((own, lat), jnp.float32)
         return carry
 
-    copies = exchange(first_out, first_in, 0)
-    for copy in copies:
-        copy.start()
     lax.fori_loop(0, levels, clear, 0)
-    for copy in copies:
-        copy.wait()
-    unpack_fields(first_in)
-
-    def unpack_material(q, carry):
-        for f in range(3):
-            def put(j, tile, f=f):
-                mat[f, q * 4 + j, own:own + TILE, :] = tile
-
-            unpack(first_in[0, 9 + f, q], first_in[1, 9 + f, q], put)
-        return carry
-
-    lax.fori_loop(0, quads, unpack_material, 0)
-
-    for epoch in range(-(-steps // HALO)):
-        if epoch:
-            pack_fields(next_out.at[epoch - 1])
-            copies = exchange(next_out.at[epoch - 1], next_in.at[epoch - 1], epoch)
-            for copy in copies:
-                copy.start()
-            for copy in copies:
-                copy.wait()
-            unpack_fields(next_in.at[epoch - 1])
-        lax.fori_loop(epoch * HALO, min((epoch + 1) * HALO, steps - 1), step, 0)
-
-    sweep(velocity_level)
-    last = steps - 1
-    fwd_copy(last).wait()
-
-    def last_levels(owner, write):
-        for j in range(share):
-            z = owner * share + j
-            for r, n in blocks[:-1]:
-                v, e, tr = rates(z, r, n)
-                for i, term in enumerate(terms(last, z, r, n, v, e, tr)):
-                    write(i, j, z, r, n, acc[i, z, r:r + n, :] + term)
-
-    def red_copy(d, owner):
+
+    def red_copy(d):
         return pltpu.make_async_remote_copy(
             src_ref=red_out.at[d], dst_ref=red_in.at[d],
             send_sem=red_send.at[d], recv_sem=red_recv.at[d],
-            device_id=(owner, me_l), device_id_type=pl.DeviceIdType.MESH,
-        )
-
-    def send_levels(d, carry):
-        owner = lax.rem(me_e + d + 1, events)
-
-        def write(i, j, z, r, n, total):
-            red_out[d, i, j, r:r + n, :] = total.astype(jnp.bfloat16)
-
-        last_levels(owner, write)
-        red_copy(d, owner).start()
+            device_id=(lax.rem(me_e + d, events), me_l), device_id_type=pl.DeviceIdType.MESH,
+        )
+
+    def velocities(i):
+        @pl.when((i >= 0) & (i < quads))
+        def _():
+            for j in range(GROUP):
+                velocity_level(quad_of(i) * GROUP + j)
+
+    def stresses(t, i, then):
+        @pl.when((i >= 0) & (i < quads))
+        def _():
+            @pl.when(i == 0)
+            def _():
+                fwd_copy(t).wait()
+
+            for j in range(GROUP):
+                stress_level(t, quad_of(i) * GROUP + j)
+            then(i)
+
+    def totals(t, i):
+        @pl.when((i >= 0) & (i < quads))
+        def _():
+            @pl.when(i == 0)
+            def _():
+                fwd_copy(t).wait()
+
+            for part in range(GROUP // share):
+                owner = quad_of(i) * (GROUP // share) + part
+                d = lax.rem(owner - me_e + events, events)
+                for j in range(share):
+                    z = owner * share + j
+                    for r, n in blocks[:-1]:
+                        v, e, tr = rates(z, r, n)
+                        for k, term in enumerate(terms(t, z, r, n, v, e, tr)):
+                            total = acc[k, z, r:r + n, :] + term
+                            red_out[d, k, j, r:r + n, :] = total.astype(jnp.bfloat16)
+
+                @pl.when(d != 0)
+                def _():
+                    red_copy(d).start()
+
+    epochs = -(-steps // HALO)
+    for epoch in range(epochs):
+        first, count = epoch * HALO, min(HALO, steps - epoch * HALO)
+        final = epoch == epochs - 1
+        full = count - 1 if final else count
+
+        def send_edges(s, i, epoch=epoch, count=count):
+            @pl.when(s == count - 1)
+            def _():
+                pack_fields(next_out.at[epoch], i, quad_of(i))
+                for copy in exchange(next_out.at[epoch], next_in.at[epoch], epoch + 1, i):
+                    copy.start()
+
+        def slot(k, carry, epoch=epoch, first=first, full=full, final=final, send=send_edges):
+            @pl.when(k < quads)
+            def _():
+                receive(epoch, k)
+
+            k = k - 1
+
+            def half_steps(s, carry):
+                velocities(k - 2 * s)
+                stresses(
+                    first + s, k - 2 * s - 1, (lambda i: None) if final else lambda i: send(s, i)
+                )
+                return carry
+
+            low = jnp.maximum(0, (k - quads + 1) // 2)
+            high = jnp.minimum(full, (k + 2) // 2)
+            lax.fori_loop(low, jnp.maximum(low, high), half_steps, 0)
+            if final:
+                velocities(k - 2 * full)
+                totals(first + full, k - 2 * full - 1)
+            return carry
+
+        lax.fori_loop(0, quads + 2 * count, slot, 0)
+
+    def finish(i, carry):
+        for epoch in range(epochs):
+            src, dst = (first_out, first_in) if epoch == 0 else (
+                next_out.at[epoch - 1], next_in.at[epoch - 1]
+            )
+            for copy in exchange(src, dst, epoch, i):
+                copy.wait_send()
         return carry
 
-    lax.fori_loop(0, events - 1, send_levels, 0)
-
-    def keep(i, j, z, r, n, total):
-        acc[i, z, r:r + n, :] = total
-
-    last_levels(me_e, keep)
+    lax.fori_loop(0, quads, finish, 0)
 
     def finish_copies(d, carry):
-        red_copy(d, lax.rem(me_e + d + 1, events)).wait()
+        red_copy(d).wait()
         return carry
 
-    lax.fori_loop(0, events - 1, finish_copies, 0)
+    lax.fori_loop(1, events, finish_copies, 0)
 
     for j in range(share):
         z = me_e * share + j
         for r, n in blocks[:-1]:
             k_lame, half_shear, k_dens = (
-                acc[i, z, r:r + n, :]
-                + sum(red_in[d, i, j, r:r + n, :].astype(jnp.float32) for d in range(events - 1))
+                red_out[0, i, j, r:r + n, :].astype(jnp.float32)
+                + sum(red_in[d, i, j, r:r + n, :].astype(jnp.float32) for d in range(1, events))
                 for i in range(3)
             )
             k_shear = 2.0 * half_shear
@@ -334,10 +354,10 @@
     levels, own, lat = p_speed.shape
     steps = forward_state.shape[1]
     events = lax.axis_size("event")
-    share, quads = levels // events, levels // 4
+    share, quads = levels // events, levels // GROUP
     epochs = -(-steps // HALO)
     f32, bf16 = jnp.float32, jnp.bfloat16
-    anywhere = pl.BlockSpec(memory_space=pl.ANY)
+    anywhere = pl.BlockSpec(memory_space=pltpu.HBM)
     return pl.pallas_call(
         kernel,
         out_shape=jax.ShapeDtypeStruct((3, share, own, lat), f32),
@@ -352,21 +372,21 @@
             pltpu.VMEM((9, levels + 2, PAD + own + 2 * TILE, lat), f32),
             pltpu.VMEM((3, levels, own + TILE, lat), f32),
             pltpu.VMEM((3, levels, own, lat), f32),
-            pltpu.VMEM((2, 12, quads, 2 * TILE, lat), bf16),
-            pltpu.VMEM((2, 12, quads, 2 * TILE, lat), bf16),
-            pltpu.VMEM((max(epochs - 1, 1), 2, 9, quads, 2 * TILE, lat), bf16),
-            pltpu.VMEM((max(epochs - 1, 1), 2, 9, quads, 2 * TILE, lat), bf16),
-            pltpu.VMEM((events - 1, 3, share, own, lat), bf16),
-            pltpu.VMEM((events - 1, 3, share, own, lat), bf16),
+            pltpu.VMEM((quads, 2, 12, 2 * TILE, lat), bf16),
+            pltpu.VMEM((quads, 2, 12, 2 * TILE, lat), bf16),
+            pltpu.VMEM((max(epochs - 1, 1), quads, 2, 9, 2 * TILE, lat), bf16),
+            pltpu.VMEM((max(epochs - 1, 1), quads, 2, 9, 2 * TILE, lat), bf16),
+            pltpu.VMEM((events, 3, share, own, lat), bf16),
+            pltpu.VMEM((events, 3, share, own, lat), bf16),
             pltpu.SemaphoreType.DMA((4,)),
             pltpu.SemaphoreType.DMA((steps,)),
-            pltpu.SemaphoreType.DMA((epochs, 2)),
-            pltpu.SemaphoreType.DMA((epochs, 2)),
-            pltpu.SemaphoreType.DMA((events - 1,)),
-            pltpu.SemaphoreType.DMA((events - 1,)),
+            pltpu.SemaphoreType.DMA((epochs, quads, 2)),
+            pltpu.SemaphoreType.DMA((epochs, quads, 2)),
+            pltpu.SemaphoreType.DMA((events,)),
+            pltpu.SemaphoreType.DMA((events,)),
         ],
         compiler_params=pltpu.CompilerParams(
-            collective_id=0, has_side_effects=True, vmem_limit_bytes=40 * 2**20
+            collective_id=0, has_side_effects=True, vmem_limit_bytes=60 * 2**20
         ),
         name="adjoint",
     )(adjoint_init, forward_state, p_speed, s_speed, density)

time: 50.5 us -> 36 us (0.71)
  Pallas kernels: 41.8 us -> 34.3 us
  local copies, waits for them, and re-layouts: 8.44 us -> 1.54 us
    pallas_call x1, Pallas kernels: 41.8 us -> 34.3 us  [shards(): pl.pallas_call(kernel, out_shape=jax.ShapeDtypeStruct((3, share, own, lat...]
    unnamed x11 -> x1, local copies, waits for them, and re-layouts: 8.44 us -> 1.54 us
where the time goes in v2:
time: 36 us; the launch traced here: 35.9 us
  Pallas kernels  34.3 us (95%)
  local copies, waits for them, and re-layouts  1.54 us (4%)
    pallas_call x1, Pallas kernels, shards(): pl.pallas_call(kernel, out_shape=jax.ShapeDtypeStruct((3, share, own, lat...  34.3 us
    unnamed x1, local copies, waits for them, and re-layouts  1.54 us

profile of v2, /device:TPU:0, one launch (start us, length us, event | category | flops | bytes accessed | tf_op | source)
XLA Modules:
  0.0 35.9 jit_solution(7134418025550928917)
XLA Ops:
  0.0 34.3 %adjoint.1 = f32[3,2,32,128]{3,2,1,0:T(8,128)} custom-call(bf16[1,9,16,32,128]{4,3,2,1,0:T(8,128)(2,1)} %adj_hbm.1, bf16[1,8,9,16,32,128]{5,4,3,2,1,0:T(8,128)(2,1)} %fwd_hbm.1, f32[16,32,128]{2,1,0:T(8,128)} %p_hbm.1, f32[16,32,128]{2,1,0:T(8,128)} %s_hbm.1, f32[16,32,128]{2,1,0:T(8,128)} %d_hbm.1), custom_call_target="tpu_custom_call" | custom-call | tf_op jit(solution)/shard_map/adjoint/pallas_call | solution.py:361
  34.3 1.5 %copy.7 = f32[3,2,32,128]{3,2,1,0:T(8,128)} copy(f32[3,2,32,128]{3,2,1,0:T(8,128)} %adjoint.1) | data formatting | bytes 196608

commit v3 on v2

--- a/solution.py
+++ b/solution.py
@@ -38,14 +38,28 @@
     right, left = lax.rem(me_l + 1, ring), lax.rem(me_l + ring - 1, ring)
     share = levels // events
 
-    local = [
-        pltpu.make_async_copy(src, dst, local_sem.at[i])
-        for i, (src, dst) in enumerate(
-            ((adj_hbm.at[0], adj), (d_hbm, d_raw), (p_hbm, p_raw), (s_hbm, s_raw))
-        )
-    ]
-    for copy in local:
-        copy.start()
+    quads = levels // GROUP
+    flip = jnp.where(me_e * 2 < events, 1, 0)
+
+    def quad_of(i):
+        return i + flip * (quads - 1 - 2 * i)
+
+    def local_copies(i):
+        rows = pl.ds(quad_of(i) * GROUP, GROUP)
+        pairs = (
+            (adj_hbm.at[0, :, rows], adj.at[:, rows]),
+            (d_hbm.at[rows], d_raw.at[rows]),
+            (p_hbm.at[rows], p_raw.at[rows]),
+            (s_hbm.at[rows], s_raw.at[rows]),
+        )
+        return [
+            pltpu.make_async_copy(src, dst, local_sem.at[i, k])
+            for k, (src, dst) in enumerate(pairs)
+        ]
+
+    for i in range(quads):
+        for copy in local_copies(i):
+            copy.start()
 
     def fwd_copy(t):
         return pltpu.make_async_copy(fwd_hbm.at[0, t], fwd.at[t], fwd_sem.at[t])
@@ -88,12 +102,6 @@
             r, l = (v[half * TILE:(half + 1) * TILE] for v in (r16, l16))
             put(2 * half, jnp.where(upper, r, pltpu.roll(l, HALO, 0)))
             put(2 * half + 1, jnp.where(upper, pltpu.roll(r, HALO, 0), l))
-
-    quads = levels // GROUP
-    flip = jnp.where(me_e * 2 < events, 1, 0)
-
-    def quad_of(i):
-        return i + flip * (quads - 1 - 2 * i)
 
     def exchange(src, dst, at, i):
         return [
@@ -112,13 +120,13 @@
 
             pack(lambda j, r, f=f: w[f, q * GROUP + j + 1, PAD + r:PAD + r + TILE, :], put)
 
-    for copy in local:
-        copy.wait()
     for t in range(steps):
         fwd_copy(t).start()
 
     def prepare(i, carry):
         q = quad_of(i)
+        for copy in local_copies(i):
+            copy.wait()
         for j in range(GROUP):
             z = q * GROUP + j
             d, p, s = d_raw[z], p_raw[z], s_raw[z]
@@ -169,36 +177,46 @@
 
     blocks = [(r, 2 * TILE) for r in range(0, own, 2 * TILE)] + [(own, TILE)]
 
-    def velocity_level(z):
+    def velocity_levels(q):
         for r, n in blocks:
-            def ld(f, off=0, dz=0):
-                return w[f, z + 1 + dz, pl.ds(PAD + r + off, n), :]
-
-            buoy = mat[0, z, r:r + n, :]
-            xy, xz, yz, zz = ld(XY), ld(XZ), ld(YZ), ld(ZZ)
-            fx = (ld(XX, 1) - ld(XX)) + behind_lat(xy) + (xz - ld(XZ, 0, -1))
-            fy = (xy - ld(XY, -1)) + ahead_lat(ld(YY)) + (yz - ld(YZ, 0, -1))
-            fz = (xz - ld(XZ, -1)) + behind_lat(yz) + (ld(ZZ, 0, 1) - zz)
-            for f, force in ((VX, fx), (VY, fy), (VZ, fz)):
-                v = ld(f) + buoy * force
-                w[f, z + 1, PAD + r:PAD + r + n, :] = v
-                if r == 0 and f in (VY, VZ):
-                    w[f, z + 1, PAD + own + TILE:PAD + own + 2 * TILE, :] = v[:TILE]
-                if r == own and f == VX:
-                    w[f, z + 1, 0:TILE, :] = v
-
-    def rates(z, r, n):
+            below = None
+            for j in range(GROUP):
+                z = q * GROUP + j
+
+                def ld(f, off=0, dz=0):
+                    return w[f, z + 1 + dz, pl.ds(PAD + r + off, n), :]
+
+                if j == 0:
+                    below = (ld(XZ, 0, -1), ld(YZ, 0, -1))
+                    zz = ld(ZZ)
+                buoy = mat[0, z, r:r + n, :]
+                xy, xz, yz, above = ld(XY), ld(XZ), ld(YZ), ld(ZZ, 0, 1)
+                fx = (ld(XX, 1) - ld(XX)) + behind_lat(xy) + (xz - below[0])
+                fy = (xy - ld(XY, -1)) + ahead_lat(ld(YY)) + (yz - below[1])
+                fz = (xz - ld(XZ, -1)) + behind_lat(yz) + (above - zz)
+                below, zz = (xz, yz), above
+                for f, force in ((VX, fx), (VY, fy), (VZ, fz)):
+                    v = ld(f) + buoy * force
+                    w[f, z + 1, PAD + r:PAD + r + n, :] = v
+                    if r == 0 and f in (VY, VZ):
+                        w[f, z + 1, PAD + own + TILE:PAD + own + 2 * TILE, :] = v[:TILE]
+                    if r == own and f == VX:
+                        w[f, z + 1, 0:TILE, :] = v
+
+    def rates(z, r, n, held):
         def ld(f, off=0, dz=0):
             return w[f, z + 1 + dz, pl.ds(PAD + r + off, n), :]
 
-        vx, vy, vz = ld(VX), ld(VY), ld(VZ)
+        vx, vy, behind = held or (ld(VX), ld(VY), ld(VZ, 0, -1))
+        vz, above_x, above_y = ld(VZ), ld(VX, 0, 1), ld(VY, 0, 1)
         exx = vx - ld(VX, -1)
         eyy = behind_lat(vy)
-        ezz = vz - ld(VZ, 0, -1)
+        ezz = vz - behind
         gxy = ahead_lat(vx) + (ld(VY, 1) - vy)
-        gxz = (ld(VX, 0, 1) - vx) + (ld(VZ, 1) - vz)
-        gyz = (ld(VY, 0, 1) - vy) + ahead_lat(vz)
-        return (vx, vy, vz), (exx, eyy, ezz, gxy, gxz, gyz), exx + eyy + ezz
+        gxz = (above_x - vx) + (ld(VZ, 1) - vz)
+        gyz = (above_y - vy) + ahead_lat(vz)
+        held = (above_x, above_y, vz)
+        return (vx, vy, vz), (exx, eyy, ezz, gxy, gxz, gyz), exx + eyy + ezz, held
 
     def terms(t, z, r, n, v, e, tr):
         F = [fwd[t, f, z, r:r + n, :].astype(jnp.float32) for f in range(9)]
@@ -209,23 +227,26 @@
         k_dens = v[0] * F[0] + v[1] * F[1] + v[2] * F[2]
         return k_lame, half_shear, k_dens
 
-    def stress_level(t, z):
+    def stress_levels(t, q):
         for r, n in blocks:
-            v, e, tr = rates(z, r, n)
-            lame, shear = mat[1, z, r:r + n, :], mat[2, z, r:r + n, :]
-            volume, twice = lame * tr, shear + shear
-            for i, f in enumerate((XX, YY, ZZ, XY, XZ, YZ)):
-                rows = slice(PAD + r, PAD + r + n)
-                s = w[f, z + 1, rows, :]
-                s = (s + volume) + twice * e[i] if i < 3 else s + shear * e[i]
-                w[f, z + 1, rows, :] = s
-                if r == 0 and f == XX:
-                    w[f, z + 1, PAD + own + TILE:PAD + own + 2 * TILE, :] = s[:TILE]
-                if r == own and f in (XY, XZ):
-                    w[f, z + 1, 0:TILE, :] = s
-            if r < own:
-                for i, term in enumerate(terms(t, z, r, n, v, e, tr)):
-                    acc[i, z, r:r + n, :] += term
+            held = None
+            for j in range(GROUP):
+                z = q * GROUP + j
+                v, e, tr, held = rates(z, r, n, held)
+                lame, shear = mat[1, z, r:r + n, :], mat[2, z, r:r + n, :]
+                volume, twice = lame * tr, shear + shear
+                for i, f in enumerate((XX, YY, ZZ, XY, XZ, YZ)):
+                    rows = slice(PAD + r, PAD + r + n)
+                    s = w[f, z + 1, rows, :]
+                    s = (s + volume) + twice * e[i] if i < 3 else s + shear * e[i]
+                    w[f, z + 1, rows, :] = s
+                    if r == 0 and f == XX:
+                        w[f, z + 1, PAD + own + TILE:PAD + own + 2 * TILE, :] = s[:TILE]
+                    if r == own and f in (XY, XZ):
+                        w[f, z + 1, 0:TILE, :] = s
+                if r < own:
+                    for i, term in enumerate(terms(t, z, r, n, v, e, tr)):
+                        acc[i, z, r:r + n, :] += term
 
     def clear(z, carry):
         for i in range(3):
@@ -244,8 +265,7 @@
     def velocities(i):
         @pl.when((i >= 0) & (i < quads))
         def _():
-            for j in range(GROUP):
-                velocity_level(quad_of(i) * GROUP + j)
+            velocity_levels(quad_of(i))
 
     def stresses(t, i, then):
         @pl.when((i >= 0) & (i < quads))
@@ -254,8 +274,7 @@
             def _():
                 fwd_copy(t).wait()
 
-            for j in range(GROUP):
-                stress_level(t, quad_of(i) * GROUP + j)
+            stress_levels(t, quad_of(i))
             then(i)
 
     def totals(t, i):
@@ -268,10 +287,11 @@
             for part in range(GROUP // share):
                 owner = quad_of(i) * (GROUP // share) + part
                 d = lax.rem(owner - me_e + events, events)
-                for j in range(share):
-                    z = owner * share + j
-                    for r, n in blocks[:-1]:
-                        v, e, tr = rates(z, r, n)
+                for r, n in blocks[:-1]:
+                    held = None
+                    for j in range(share):
+                        z = owner * share + j
+                        v, e, tr, held = rates(z, r, n, held)
                         for k, term in enumerate(terms(t, z, r, n, v, e, tr)):
                             total = acc[k, z, r:r + n, :] + term
                             red_out[d, k, j, r:r + n, :] = total.astype(jnp.bfloat16)
@@ -378,7 +398,7 @@
             pltpu.VMEM((max(epochs - 1, 1), quads, 2, 9, 2 * TILE, lat), bf16),
             pltpu.VMEM((events, 3, share, own, lat), bf16),
             pltpu.VMEM((events, 3, share, own, lat), bf16),
-            pltpu.SemaphoreType.DMA((4,)),
+            pltpu.SemaphoreType.DMA((quads, 4)),
             pltpu.SemaphoreType.DMA((steps,)),
             pltpu.SemaphoreType.DMA((epochs, quads, 2)),
             pltpu.SemaphoreType.DMA((epochs, quads, 2)),

time: 36 us -> 35.8 us (level)
  no operation moved by 1% of the time
where the time goes in v3:
time: 35.8 us; the launch traced here: 35.6 us
  Pallas kernels  34.1 us (95%)
  local copies, waits for them, and re-layouts  1.54 us (4%)
    pallas_call x1, Pallas kernels, shards(): pl.pallas_call(kernel, out_shape=jax.ShapeDtypeStruct((3, share, own, lat...  34.1 us
    unnamed x1, local copies, waits for them, and re-layouts  1.54 us

profile of v3, /device:TPU:0, one launch (start us, length us, event | category | flops | bytes accessed | tf_op | source)
XLA Modules:
  0.0 35.6 jit_solution(6405451259342493337)
XLA Ops:
  0.0 34.1 %adjoint.1 = f32[3,2,32,128]{3,2,1,0:T(8,128)} custom-call(bf16[1,9,16,32,128]{4,3,2,1,0:T(8,128)(2,1)} %adj_hbm.1, bf16[1,8,9,16,32,128]{5,4,3,2,1,0:T(8,128)(2,1)} %fwd_hbm.1, f32[16,32,128]{2,1,0:T(8,128)} %p_hbm.1, f32[16,32,128]{2,1,0:T(8,128)} %s_hbm.1, f32[16,32,128]{2,1,0:T(8,128)} %d_hbm.1), custom_call_target="tpu_custom_call" | custom-call | tf_op jit(solution)/shard_map/adjoint/pallas_call | solution.py:381
  34.1 1.5 %copy.7 = f32[3,2,32,128]{3,2,1,0:T(8,128)} copy(f32[3,2,32,128]{3,2,1,0:T(8,128)} %adjoint.1) | data formatting | bytes 196608
